TPU v7x, 32 devices: a whole 2x2x4 slice. The times are simulated.
32 devices in a mesh: gz: 16 (over z, x, core), ph: 2 (over y).
Axes of the slice: x: 2, y: 2, z: 4, core: 2. Of those that a mesh axis runs over, the one named last changes fastest.
Arguments:
- frac: bfloat16 [2, 128, 64, 256], P('ph', 'gz'), may hold values from 0.0099487305 to 0.099609375
- velocity: bfloat16 [2, 3, 128, 64, 256], P('ph', None, 'gz'), may hold values from -6 to 6
- gas_vel: bfloat16 [3, 128, 64, 256], P(None, 'gz'), may hold values from -6 to 6
- diameters: float32 [32], replicated, may hold values from 0.5 to 4
- phase_map: int32 [2], P('ph'), may hold values from 0 to 31
- wall_mask: int32 [64, 256], replicated, may hold values 0 or 1
- offsets: int32 [128], replicated, may hold values from 0 to 255
Outputs:
- pressure: float32 [128, 64, 256], P('gz')
- corrected: bfloat16 [2, 3, 128, 64, 256], P('ph', None, 'gz')
Inputs may be any that keep to these rules, and one draw needn't show every extreme that they name: `wall_mask`: 1 marks a fluid cell, 0 a lifter or wall cell.
All inputs are finite; a program needn't handle non-finite values.
Results may differ from a plain program's by a relative error of at most 0.001.
Values sent between devices are 32-bit elements; how exact they have to be, the bound alone decides.
A program may use at most 64 MiB of HBM per device.

v0:
```python
import math

import jax
import jax.numpy as jnp
from jax import lax
from jax.sharding import PartitionSpec as P

DT_STEP = 0.5
DRAG_SCALE = 20.0
COMPRESS = 0.005
HIGHEST = lax.Precision.HIGHEST


def from_behind(block, axis, distance):
    devices = range(lax.axis_size(axis))
    route = [((i - distance) % len(devices), i) for i in devices]
    return lax.ppermute(block, axis, route)


def real_basis(count):
    index_rows = jnp.arange(count, dtype=jnp.int32)[:, None]
    column = jnp.arange(count, dtype=jnp.int32)[None, :]
    half = count // 2
    wave = jnp.where(column <= half, column, column - half)
    angle = 2.0 * math.pi / count * (index_rows * wave % count).astype(jnp.float32)
    scaled = math.sqrt(2.0 / count)
    cosine = jnp.cos(angle)
    table = jnp.where(column < half, scaled * cosine, scaled * jnp.sin(angle))
    return jnp.where((column == 0) | (column == half), cosine / math.sqrt(count), table)


def eigen_values(count):
    column = jnp.arange(count, dtype=jnp.int32)
    half = count // 2
    wave = jnp.where(column <= half, column, column - half).astype(jnp.float32)
    return 2.0 - 2.0 * jnp.cos(2.0 * math.pi / count * wave)


def rotate_mask(wall_mask, turns, around_count):
    around_idx = (
        jnp.arange(around_count, dtype=jnp.int32)[None, :] - turns[:, None]
    ) % around_count
    return jnp.transpose(jnp.take(wall_mask, around_idx, axis=1), (1, 0, 2)).astype(jnp.float32)


def radial_solve(spectral, axial_eig, theta_eig, radius_vec, angle_step):
    radial_count = radius_vec.shape[0]
    inner = radius_vec - 0.5
    outer = jnp.where(jnp.arange(radial_count) == radial_count - 1, 0.0, radius_vec + 0.5)
    diag = (
        COMPRESS
        + axial_eig[:, None, None]
        + theta_eig[None, :, None] / (radius_vec * angle_step) ** 2
        + ((outer + inner) / radius_vec)[None, None, :]
    )
    lower = jnp.broadcast_to(-inner / radius_vec, diag.shape)
    upper = jnp.broadcast_to(-outer / radius_vec, diag.shape)
    right = -jnp.transpose(spectral, (0, 2, 1))[..., None]
    solved = lax.linalg.tridiagonal_solve(lower, diag, upper, right)[..., 0]
    return jnp.transpose(solved, (0, 2, 1))


def to_space(modes, around_table):
    return jnp.dot(
        modes.reshape(-1, around_table.shape[0]), around_table.T, precision=HIGHEST
    ).reshape(modes.shape)


def shards(frac, velocity, gas_vel, diameters, phase_map, wall_mask, offsets):
    plane_count = frac.shape[1]
    radial_count = frac.shape[2]
    around_count = frac.shape[3]
    axial_total = offsets.shape[0]
    phase_count = lax.axis_size("ph")
    slab_index = lax.axis_index("gz")
    first_plane = slab_index * plane_count
    angle_step = 2.0 * math.pi / around_count
    plane_ids = (first_plane + jnp.arange(plane_count + 1, dtype=jnp.int32)) % axial_total
    fluid_all = rotate_mask(wall_mask, jnp.take(offsets, plane_ids), around_count)
    fluid = fluid_all[:plane_count]
    open_radial = fluid * jnp.concatenate([fluid[:, 1:], jnp.zeros_like(fluid[:, :1])], 1)
    open_around = fluid * jnp.roll(fluid, -1, 2)
    open_axial = fluid * fluid_all[1:]
    radius_vec = jnp.arange(radial_count, dtype=jnp.float32) + 0.5
    radii = radius_vec[:, None]
    which = (jnp.arange(diameters.shape[0], dtype=jnp.int32) == phase_map[0]).astype(jnp.float32)
    size_here = jnp.sum(diameters * which)
    volume = frac[0].astype(jnp.float32)
    gas = gas_vel.astype(jnp.float32)
    slip = velocity[0].astype(jnp.float32) - gas
    speed = jnp.sqrt(1.0 + jnp.sum(slip * slip, 0))
    beta = DRAG_SCALE * volume / (size_here * size_here) * (1.0 + 0.15 * speed)
    relax = 1.0 / (1.0 + DT_STEP * beta)
    predicted = gas + relax * slip
    share = volume * relax * slip + gas / phase_count
    flux_radial = share[0] * open_radial
    flux_around = share[1] * open_around
    flux_axial = share[2] * open_axial
    below = from_behind(flux_axial[-1:], "gz", 1)
    axial_prev = jnp.concatenate([below, flux_axial[:-1]], 0)
    radial_prev = jnp.concatenate([jnp.zeros_like(flux_radial[:, :1]), flux_radial[:, :-1]], 1)
    term = ((radii + 0.5) * flux_radial - (radii - 0.5) * radial_prev) / radii
    term = term + (flux_around - jnp.roll(flux_around, 1, 2)) / (radii * angle_step)
    term = (term + flux_axial - axial_prev) / DT_STEP
    around_table = real_basis(around_count)
    axial_table = real_basis(axial_total)
    axial_eig = eigen_values(axial_total)
    axial_step = None
    source = lax.psum(term, "ph")
    modes = jnp.dot(source.reshape(-1, around_count), around_table, precision=HIGHEST).reshape(
        source.shape
    )
    pencil = lax.all_to_all(modes, "gz", split_axis=2, concat_axis=0, tiled=True)
    mode_count = pencil.shape[2]
    theta_eig = lax.dynamic_slice_in_dim(
        eigen_values(around_count), slab_index * mode_count, mode_count
    )
    flat = pencil.reshape(axial_total, -1)
    spectral = jnp.dot(axial_table.T, flat, precision=HIGHEST).reshape(pencil.shape)
    solved = radial_solve(spectral, axial_eig, theta_eig, radius_vec, angle_step)
    space = jnp.dot(axial_table, solved.reshape(axial_total, -1), precision=HIGHEST).reshape(
        pencil.shape
    )
    ahead = jnp.roll(space, -1, 0) - space
    back, back_step = (
        lax.all_to_all(space, "gz", split_axis=0, concat_axis=2, tiled=True),
        lax.all_to_all(ahead, "gz", split_axis=0, concat_axis=2, tiled=True),
    )
    pressure = to_space(back, around_table)
    axial_step = to_space(back_step, around_table)
    radial_step = (jnp.concatenate([pressure[:, 1:], pressure[:, -1:]], 1) - pressure) * open_radial
    around_step = (jnp.roll(pressure, -1, 2) - pressure) / (radii * angle_step) * open_around
    gradient = jnp.stack([radial_step, around_step, axial_step * open_axial])
    corrected = (predicted - DT_STEP * gradient).astype(jnp.bfloat16)[None]
    return (pressure, corrected)


def solution(mesh):
    in_specs = (
        P("ph", "gz", None, None),
        P("ph", None, "gz", None, None),
        P(None, "gz", None, None),
        P(),
        P("ph"),
        P(),
        P(),
    )
    out_specs = (P("gz", None, None), P("ph", None, "gz", None, None))
    return jax.shard_map(shards, mesh=mesh, in_specs=in_specs, out_specs=out_specs, check_vma=False)
```

profile of v0, /device:TPU:0, one launch (start us, length us, event | category | flops | bytes accessed | tf_op | source)
XLA Modules:
  0.0 302.2 jit_solution(15533590216311717967)
XLA Ops:
  7.3 0.6 copy-done
  7.8 0.7 gather_fusion
  8.7 0.9 copy.313
  9.6 3.9 %gather_fusion.1 = s32[2304,64]{1,0:T(8,128)S(1)} fusion(s32[64,256]{0,1:T(8,128)S(1)} %copy.313, s32[3072]{0:T(1024)S(1)} %pad_clamp_fusion), kind=kCustom, calls=%fused_computation.1 | custom fusion | bytes 1188864 | tf_op jit(solution)/shard_map/jit(_take)/gather | solution.py:43
  13.6 0.3 copy.315
  15.5 0.6 fusion.184
  17.7 0.7 copy-done.14
  18.4 1.1 fusion.219
  19.5 0.3 fusion
  19.8 0.4 fusion.14
  20.2 0.6 collective-permute-start
  21.1 0.7 fusion.271
  21.8 0.7 fusion.270
  22.4 5.2 %collective-permute-done = f32[1,64,256]{2,1,0:T(8,128)S(1)} collective-permute-done((f32[1,64,256]{2,1,0:T(8,128)S(1)}, f32[1,64,256]{2,1,0:T(8,128)S(1)}, u32[]{:S(2)}, u32[]{:S(2)}) %collective-permute-start) | collective-permute-done | bytes 65568 | tf_op jit(solution)/shard_map/ppermute | solution.py:17
  27.7 1.2 fusion.19
  28.9 0.7 fusion.269
  29.6 0.7 fusion.268
  30.3 0.7 fusion.266
  31.1 0.7 fusion.267
  31.8 24.9 %all-reduce.4.cloned.1.call-done = f32[8,64,256]{2,1,0:T(8,128)} async-done(((f32[8,64,256]{2,1,0:T(8,128)}), f32[8,64,256]{2,1,0:T(8,128)}) %all-reduce.4.cloned.1.call-update) | async-done | bytes 524304 | tf_op jit(solution)/shard_map/psum | solution.py:109
  56.7 3.5 %fusion.32 = f32[8,64,256]{2,1,0:T(8,128)} fusion(f32[8,64,256]{2,1,0:T(8,128)} %all-reduce.4.cloned.1.call-done, s32[256]{0:T(256)S(1)} %compare_select_fusion.2, pred[256]{0:T(512)(128)(4,1)S(1)} %get-tuple-element.424, pred[256]{0:T(512)(128)(4,1)S(1)} %get-tuple-element.423), kind=kOutput, calls=%fused_computation.61 | convolution fusion | flops 403898368 | bytes 1050112 | tf_op jit(solution)/shard_map/dot_general | solution.py:110
  60.2 1.5 copy.316
  61.7 1.4 reshape.6226
  63.2 5.6 %all-to-all-start = ((f32[16,1,8192]{2,1,0:T(1,128)}), f32[16,1,8192]{2,1,0:T(1,128)S(1)}, u32[]{:S(2)}, u32[]{:S(2)}) async-start(f32[16,1,8192]{2,1,0:T(1,128)} %reshape.6226), calls=%async_computation | async-start | bytes 1048576 | tf_op jit(solution)/shard_map/all_to_all | solution.py:113
  68.9 0.7 fusion.265
  69.6 0.7 fusion.264
  70.7 0.9 slice_bitcast_fusion.4
  71.6 11.4 %all-to-all-done = f32[16,1,8192]{2,1,0:T(1,128)S(1)} async-done(((f32[16,1,8192]{2,1,0:T(1,128)}), f32[16,1,8192]{2,1,0:T(1,128)S(1)}, u32[]{:S(2)}, u32[]{:S(2)}) %all-to-all-start) | async-done | bytes 524320 | tf_op jit(solution)/shard_map/all_to_all | solution.py:113
  83.0 0.5 broadcast.5623
  83.5 2.7 reduce.4
  86.2 1.5 reshape.6227
  87.7 2.7 copy.318
  90.4 4.7 %reshape.6196 = f32[128,1024]{1,0:T(8,128)S(1)} reshape(f32[16,8,64,16]{3,2,1,0:T(8,128)} %copy.318) | data formatting | bytes 1048576 | tf_op jit(solution)/shard_map/reshape | solution.py:118
  95.3 0.9 fusion.4
  96.7 0.6 copy-done.9
  97.2 77.2 %bitcast_divide_fusion.2 = (f32[128,16,1]{0,1,2:T(8,128)S(1)}, f32[128,16]{0,1:T(8,128)S(1)}, f32[128,16,1]{0,1,2:T(8,128)S(1)}, f32[128,16]{0,1:T(8,128)S(1)}, ...) fusion(f32[128,16,1]{0,1,2:T(8,128)S(1)} %bitcast.1442, ...), kind=kLoop, calls=%fused_computation.211 | loop fusion | flops 999424 | bytes 2079232 | tf_op jit(solution)/shard_map/vmap(vmap())/eval_jaxpr/div | solution.py:59
  174.4 61.8 %subtract_bitcast_fusion = (f32[128,16,1,1]{0,1,3,2:T(8,128)S(1)}, f32[128,16,1]{0,1,2:T(8,128)S(1)}, f32[128,16,1]{0,1,2:T(8,128)S(1)}, f32[128,16,1]{0,1,2:T(8...) fusion(f32[128,16,1]{0,1,2:T(8,128)S(1)} %get-tuple-element.224, ...), kind=kLoop, calls=%fused_computation.419 | loop fusion | flops 604160 | bytes 1867776 | tf_op jit(solution)/shard_map/vmap(vmap())/broadcast_in_dim | solution.py:59
  236.2 2.6 constant_dynamic-update-slice_fusion.62
  239.4 2.5 constant_dynamic-update-slice_fusion
  242.0 0.9 fusion.44
  243.1 1.5 copy.385
  244.6 2.7 reshape.6228
  247.3 4.5 %all-to-all-start.1 = ((f32[16,1,8192]{2,1,0:T(1,128)}), f32[16,1,8192]{2,1,0:T(1,128)}, u32[]{:S(2)}, u32[]{:S(2)}) async-start(f32[16,1,8192]{2,1,0:T(1,128)} %reshape.6228), calls=%async_computation.1 | async-start | bytes 1048576 | tf_op jit(solution)/shard_map/all_to_all | solution.py:126
  251.8 0.8 slice.2198
  252.6 2.1 copy.388
  254.7 0.3 slice.2046
  255.0 2.1 maximum_subtract_fusion.3
  257.1 1.6 copy.390
  258.7 1.5 reshape.6230
  260.1 5.7 %all-to-all-done.1 = f32[16,1,8192]{2,1,0:T(1,128)} async-done(((f32[16,1,8192]{2,1,0:T(1,128)}), f32[16,1,8192]{2,1,0:T(1,128)}, u32[]{:S(2)}, u32[]{:S(2)}) %all-to-all-start.1) | async-done | bytes 524320 | tf_op jit(solution)/shard_map/all_to_all | solution.py:126
  265.8 4.3 %all-to-all-start.2 = ((f32[16,1,8192]{2,1,0:T(1,128)}), f32[16,1,8192]{2,1,0:T(1,128)}, u32[]{:S(2)}, u32[]{:S(2)}) async-start(f32[16,1,8192]{2,1,0:T(1,128)} %reshape.6230), calls=%async_computation.2 | async-start | bytes 1048576 | tf_op jit(solution)/shard_map/all_to_all | solution.py:127
  270.1 3.6 %reduce.5 = f32[16,8192]{1,0:T(8,128)} reduce(f32[16,1,8192]{2,1,0:T(1,128)} %all-to-all-done.1, f32[]{:T(128)} %broadcast.5623), dimensions={1}, to_apply=%all_to_all.36.reduce_sub_computation | reduce | bytes 1048580 | tf_op jit(solution)/shard_map/all_to_all | solution.py:126
  273.7 1.5 reshape.6229
  275.3 2.7 fusion.30
  278.0 1.0 slice.2194
  279.0 1.0 slice.2196
  280.0 4.4 %all-to-all-done.2 = f32[16,1,8192]{2,1,0:T(1,128)} async-done(((f32[16,1,8192]{2,1,0:T(1,128)}), f32[16,1,8192]{2,1,0:T(1,128)}, u32[]{:S(2)}, u32[]{:S(2)}) %all-to-all-start.2) | async-done | bytes 524320 | tf_op jit(solution)/shard_map/all_to_all | solution.py:127
  284.4 2.9 reduce.6
  287.3 1.4 reshape.6231
  288.7 1.4 copy.391
  290.2 2.7 fusion.3
  293.0 0.4 fusion.21
  293.4 0.6 copy-done.13
  294.0 1.4 fusion.5
  (135 shorter events, 2.9 us)
Async XLA Ops:
  7.2 0.7 copy-start
  7.2 49.5 %all-reduce.4.cloned.1.call-start = ((), (), s32[]{:S(2)}) async-start(), calls=%async_computation.3 | async-start | bytes 1048576 | tf_op jit(solution)/shard_map/psum | solution.py:109
  14.0 1.5 copy-start.15
  14.0 3.4 %copy-start.1 = (bf16[3,8,64,256]{3,2,1,0:T(8,128)(2,1)S(1)}, bf16[3,8,64,256]{3,2,1,0:T(8,128)(2,1)}, u32[]{:S(2)}) copy-start(bf16[3,8,64,256]{3,2,1,0:T(8,128)(2,1)} %param.9) | copy-start | bytes 2359300
  14.0 3.4 %copy-start.2 = (bf16[1,3,8,64,256]{4,3,2,1,0:T(8,128)(2,1)S(1)}, bf16[1,3,8,64,256]{4,3,2,1,0:T(8,128)(2,1)}, u32[]{:S(2)}) copy-start(bf16[1,3,8,64,256]{4,3,2,1,0:T(8,128)(2,1)} %param.8) | copy-start | bytes 2359300
  14.1 5.8 %copy-start.5 = (f32[8,63,256]{2,1,0:T(8,128)}, f32[8,63,256]{2,1,0:T(8,128)S(1)}, u32[]{:S(2)}) copy-start(f32[8,63,256]{2,1,0:T(8,128)S(1)} %slice.2053) | copy-start | bytes 1548292
  14.3 5.6 %copy-start.7 = (f32[8,64,255]{2,1,0:T(8,128)}, f32[8,64,255]{2,1,0:T(8,128)S(1)}, u32[]{:S(2)}) copy-start(f32[8,64,255]{2,1,0:T(8,128)S(1)} %slice.2056) | copy-start | bytes 1566724
  17.4 1.0 copy-start.14
  20.2 7.4 %collective-permute-start = (f32[1,64,256]{2,1,0:T(8,128)S(1)}, f32[1,64,256]{2,1,0:T(8,128)S(1)}, u32[]{:S(2)}, u32[]{:S(2)}) collective-permute-start(f32[1,64,256]{2,1,0:T(8,128)S(1)} %slice.2062), channel_id=1, source_target_pairs={{30,0},{0,2},{2,4},{4,6},{6,8},{8,10},{10,12},{12,14},{14,16},{16,... | collective-permute-start | bytes 196616 | tf_op jit(solution)/shard_map/ppermute | solution.py:17
  63.2 19.9 %all-to-all-start = ((f32[16,1,8192]{2,1,0:T(1,128)}), f32[16,1,8192]{2,1,0:T(1,128)S(1)}, u32[]{:S(2)}, u32[]{:S(2)}) async-start(f32[16,1,8192]{2,1,0:T(1,128)} %reshape.6226), calls=%async_computation | async-start | bytes 1048576 | tf_op jit(solution)/shard_map/all_to_all | solution.py:113
  70.7 12.8 %copy-start.10 = (f32[128,16,64]{0,1,2:T(8,128)}, f32[128,16,64]{0,1,2:T(8,128)S(1)}, u32[]{:S(2)}) copy-start(f32[128,16,64]{0,1,2:T(8,128)S(1)} %add_add_fusion) | copy-start | bytes 1572868
  96.2 1.0 copy-start.9
  247.3 18.5 %all-to-all-start.1 = ((f32[16,1,8192]{2,1,0:T(1,128)}), f32[16,1,8192]{2,1,0:T(1,128)}, u32[]{:S(2)}, u32[]{:S(2)}) async-start(f32[16,1,8192]{2,1,0:T(1,128)} %reshape.6228), calls=%async_computation.1 | async-start | bytes 1048576 | tf_op jit(solution)/shard_map/all_to_all | solution.py:126
  265.8 18.5 %all-to-all-start.2 = ((f32[16,1,8192]{2,1,0:T(1,128)}), f32[16,1,8192]{2,1,0:T(1,128)}, u32[]{:S(2)}, u32[]{:S(2)}) async-start(f32[16,1,8192]{2,1,0:T(1,128)} %reshape.6230), calls=%async_computation.2 | async-start | bytes 1048576 | tf_op jit(solution)/shard_map/all_to_all | solution.py:127
  278.0 9.3 %copy-start.3 = (f32[8,64,256]{2,1,0:T(8,128)}, f32[8,64,256]{2,1,0:T(8,128)S(1)}, u32[]{:S(2)}) copy-start(f32[8,64,256]{2,1,0:T(8,128)S(1)} %fusion.30) | copy-start | bytes 1572868
  288.7 4.2 %copy-start.11 = (f32[8,63,256]{2,1,0:T(8,128)S(1)}, f32[8,63,256]{2,1,0:T(8,128)}, u32[]{:S(2)}) copy-start(f32[8,63,256]{2,1,0:T(8,128)} %slice.2194) | copy-start | bytes 1548292
  288.7 4.2 %copy-start.12 = (f32[8,64,255]{2,1,0:T(8,128)S(1)}, f32[8,64,255]{2,1,0:T(8,128)}, u32[]{:S(2)}) copy-start(f32[8,64,255]{2,1,0:T(8,128)} %slice.2196) | copy-start | bytes 1566724
  290.1 2.8 copy-start.4
  290.1 2.8 slice-start
  290.1 2.8 copy-start.6
  290.2 2.8 copy-start.8
  292.9 1.0 copy-start.13
Sparse Core Ops, SparseCore 0:
  29.0 27.6 all-reduce.3
where the time goes:
time: 305 us; the launch traced here: 302 us
  other arithmetic  162 us (53%)
  waiting for transfers between devices  51.7 us (17%)
  local copies, waits for them, and re-layouts  45.4 us (15%)
  between operations  17.7 us (6%)
  starting transfers between devices  14.9 us (5%)
  matrix products  10.7 us (4%)
    div x1, other arithmetic, radial_solve(): solved = lax.linalg.tridiagonal_solve(lower, diag, upper, right)[..., 0]  77.2 us
    broadcast_in_dim x1, other arithmetic, radial_solve(): solved = lax.linalg.tridiagonal_solve(lower, diag, upper, right)[..., 0]  61.8 us
    psum x1, waiting for transfers between devices, shards(): source = lax.psum(term, 'ph')  24.9 us
    unnamed x99, local copies, waits for them, and re-layouts  13.5 us
    all_to_all x1, waiting for transfers between devices, shards(): lax.all_to_all(modes, 'gz', split_axis=2, concat_axis=0, tiled=True)  11.4 us
  transfers between devices with their start and end apart: 5, of which 5 were waited for; matrix products, arithmetic and copies ran while one was open for 8% of the time, Pallas kernels for 0%

commit v1 on v0

--- a/solution.py
+++ b/solution.py
@@ -1,8 +1,12 @@
+import functools
 import math
 
 import jax
 import jax.numpy as jnp
+import numpy as np
 from jax import lax
+from jax.experimental import pallas as pl
+from jax.experimental.pallas import tpu as pltpu
 from jax.sharding import PartitionSpec as P
 
 DT_STEP = 0.5
@@ -135,6 +139,442 @@
     return (pressure, corrected)
 
 
+MESH_ID = pl.DeviceIdType.MESH
+
+
+def split_low(x):
+    high = x.astype(jnp.bfloat16)
+    return high, (x - high.astype(jnp.float32)).astype(jnp.bfloat16)
+
+
+def triple_dot(x, table_high, table_low):
+    high, low = split_low(x)
+    out = jnp.dot(high, table_high, preferred_element_type=jnp.float32)
+    out = out + jnp.dot(low, table_high, preferred_element_type=jnp.float32)
+    return out + jnp.dot(high, table_low, preferred_element_type=jnp.float32)
+
+
+def np_high_low(table):
+    high = table.astype(jnp.bfloat16)
+    low = (table - high.astype(np.float64)).astype(jnp.bfloat16)
+    return high, low
+
+
+@functools.lru_cache(maxsize=None)
+def operator_tables(radial, around, axial, planes):
+    half = around // 2
+    rows = np.arange(around)[:, None]
+    column = np.arange(around)[None, :]
+    wave = np.where(column <= half, column, column - half)
+    angle = 2.0 * np.pi / around * (rows * wave % around)
+    basis = np.sqrt(2.0 / around) * np.where(column <= half, np.cos(angle), np.sin(angle))
+    basis = np.where((column == 0) | (column == half), np.cos(angle) / np.sqrt(around), basis)
+    radius = np.arange(radial) + 0.5
+    inner = radius - 0.5
+    outer = np.where(np.arange(radial) == radial - 1, 0.0, radius + 0.5)
+    step = 2.0 * np.pi / around
+    vectors, values = [], []
+    for m in range(half + 1):
+        eig = 2.0 - 2.0 * np.cos(2.0 * np.pi / around * m)
+        matrix = np.diag((outer + inner) / radius + eig / (radius * step) ** 2)
+        off = -outer[:-1] / np.sqrt(radius[:-1] * radius[1:])
+        matrix = matrix + np.diag(off, 1) + np.diag(off, -1)
+        value, vector = np.linalg.eigh(matrix)
+        vector = vector * np.where(vector[:1] < 0.0, -1.0, 1.0)
+        values.append(value)
+        vectors.append(vector)
+    vectors = np.stack(vectors, -1)
+    values = np.maximum(np.stack(values, -1), 0.0)
+    first = vectors[:, :, :half]
+    nyquist = np.zeros((radial, max(radial, 128)))
+    nyquist[:, :radial] = vectors[:, :, half].T
+    other = np.concatenate([values[:, half:], values[:, 1:half]], -1)
+    over = COMPRESS + np.stack([values[:, :half], other])
+    root = np.sqrt(over * (over + 4.0))
+    ratio = 2.0 / (2.0 + over + root)
+    jump = ratio**planes
+    wrap = 1.0 / (1.0 - ratio**axial)
+    line = np.stack([ratio, 1.0 / root, jump, wrap], 1).astype(np.float32)
+    ahead = np_high_low(basis)
+    back = np_high_low(basis.T.copy())
+    return (
+        first.astype(np.float32),
+        nyquist.astype(np.float32),
+        line,
+        np.stack(ahead),
+        np.stack(back),
+    )
+
+
+def drum_kernel(
+    gz_count,
+    offsets_ref,
+    diameters_ref,
+    map_ref,
+    frac_ref,
+    velocity_ref,
+    gas_ref,
+    wall_ref,
+    nyquist_ref,
+    line_ref,
+    ahead_ref,
+    back_ref,
+    radial_hbm,
+    pressure_ref,
+    corrected_ref,
+    fluid,
+    pred,
+    term,
+    axial_flux,
+    halo,
+    modes,
+    partner,
+    radial,
+    radial_back,
+    lines,
+    ends_out,
+    ends_in,
+    states_out,
+    states_in,
+    solved,
+    result,
+    space,
+    table_sem,
+    halo_sem,
+    swap_send,
+    swap_recv,
+    ends_send,
+    ends_recv,
+    states_send,
+    states_recv,
+    back_send,
+    back_recv,
+):
+    me = lax.axis_index("gz")
+    ph = lax.axis_index("ph")
+    other = 1 - ph
+    planes, rows, around = term.shape
+    half = around // 2
+    axial_total = offsets_ref.shape[0]
+    blocks = rows // 8
+    angle_step = 2.0 * math.pi / around
+
+    barrier = pltpu.get_barrier_semaphore()
+    for hop in range(1, gz_count):
+        pl.semaphore_signal(
+            barrier, inc=1, device_id=(lax.rem(me + hop, gz_count), ph), device_id_type=MESH_ID
+        )
+    pl.semaphore_signal(barrier, inc=1, device_id=(me, other), device_id_type=MESH_ID)
+
+    table_copy = pltpu.make_async_copy(radial_hbm, radial, table_sem)
+    table_copy.start()
+
+    radii = lax.broadcasted_iota(jnp.int32, (rows, around), 0).astype(jnp.float32) + 0.5
+    row_id = lax.broadcasted_iota(jnp.int32, (rows, around), 0)
+    wall = wall_ref[...].astype(jnp.float32).astype(jnp.bfloat16)
+    from_col = lax.broadcasted_iota(jnp.int32, (around, around), 0)
+    to_col = lax.broadcasted_iota(jnp.int32, (around, around), 1)
+    gap = to_col - from_col
+
+    def rotate(z, carry):
+        turn = offsets_ref[lax.rem(me * planes + z, axial_total)]
+        hit = (gap == turn) | (gap == turn - around)
+        one_hot = jnp.where(hit, 1.0, 0.0).astype(jnp.bfloat16)
+        fluid[z] = jnp.dot(wall, one_hot, preferred_element_type=jnp.float32)
+        return carry
+
+    lax.fori_loop(0, planes + 1, rotate, 0)
+
+    size = diameters_ref[map_ref[0]]
+    axial_flux[0] = jnp.zeros((rows, around), jnp.float32)
+
+    def opens(z):
+        here = fluid[z]
+        open_radial = jnp.where(row_id == rows - 1, 0.0, here * pltpu.roll(here, rows - 1, 0))
+        open_around = here * pltpu.roll(here, around - 1, 1)
+        return open_radial, open_around, here * fluid[z + 1]
+
+    weight = -jnp.sqrt(radii) / DT_STEP
+    share = 1.0 / lax.axis_size("ph")
+
+    def source(z, carry):
+        volume = frac_ref[0, z].astype(jnp.float32)
+        gas = [gas_ref[a, z].astype(jnp.float32) for a in range(3)]
+        slip = [velocity_ref[0, a, z].astype(jnp.float32) - gas[a] for a in range(3)]
+        speed = jnp.sqrt(1.0 + (slip[0] * slip[0] + slip[1] * slip[1] + slip[2] * slip[2]))
+        beta = DRAG_SCALE * volume / (size * size) * (1.0 + 0.15 * speed)
+        relax = 1.0 / (1.0 + DT_STEP * beta)
+        open_radial, open_around, open_axial = opens(z)
+        for a in range(3):
+            pred[a, z] = gas[a] + relax * slip[a]
+        pull = volume * relax
+        flux_radial = (pull * slip[0] + share * gas[0]) * open_radial
+        flux_around = (pull * slip[1] + share * gas[1]) * open_around
+        flux_axial = (pull * slip[2] + share * gas[2]) * open_axial
+        axial_flux[z + 1] = flux_axial
+        out = (radii + 0.5) * flux_radial
+        inward = jnp.where(row_id == 0, 0.0, pltpu.roll(out, 1, 0))
+        total = (out - inward) / radii
+        total = total + (flux_around - pltpu.roll(flux_around, 1, 1)) / (radii * angle_step)
+        term[z] = (total + flux_axial - axial_flux[z]) * weight
+        return carry
+
+    lax.fori_loop(0, planes, source, 0)
+
+    pl.semaphore_wait(barrier, gz_count)
+
+    halo_copy = pltpu.make_async_remote_copy(
+        src_ref=axial_flux.at[planes],
+        dst_ref=halo,
+        send_sem=halo_sem.at[0],
+        recv_sem=halo_sem.at[1],
+        device_id=(lax.rem(me + 1, gz_count), ph),
+        device_id_type=MESH_ID,
+    )
+    halo_copy.start()
+
+    def swap(z):
+        return pltpu.make_async_remote_copy(
+            src_ref=modes.at[other, z],
+            dst_ref=partner.at[z],
+            send_sem=swap_send.at[z],
+            recv_sem=swap_recv.at[z],
+            device_id=(me, other),
+            device_id_type=MESH_ID,
+        )
+
+    def to_modes(z, value):
+        out = triple_dot(value, ahead_ref[0], ahead_ref[1])
+        modes[0, z] = out[:, :half]
+        modes[1, z] = out[:, half:]
+        swap(z).start()
+
+    def send_modes(k, carry):
+        to_modes(k, term[k])
+        return carry
+
+    lax.fori_loop(1, planes, send_modes, 0)
+    halo_copy.wait()
+    to_modes(0, term[0] - halo[...] * weight)
+
+    table_copy.wait()
+    is_other = jnp.where(ph == 1, 1, 0)
+    lane0 = (lax.broadcasted_iota(jnp.int32, (rows, half), 1) == 0) & (
+        jnp.broadcast_to(is_other, (rows, half)) == 1
+    )
+    for r in range(rows):
+        fill = jnp.broadcast_to(nyquist_ref[:, r : r + 1], (rows, half))
+        radial[pl.ds(r * rows, rows), :] = jnp.where(lane0, fill, radial[pl.ds(r * rows, rows), :])
+
+    def apply(table, load, z):
+        def add(k, acc):
+            for j in range(8):
+                r = k * 8 + j
+                line = jnp.broadcast_to(load(z, r), (rows, half))
+                acc = acc + table[pl.ds(pl.multiple_of(r * rows, rows), rows), :] * line
+            return acc
+
+        return lax.fori_loop(0, rows // 8, add, jnp.zeros((rows, half), jnp.float32))
+
+    def load_term(z, r):
+        return modes[ph, z, pl.ds(r, 1), :] + partner[z, pl.ds(r, 1), :]
+
+    def forward(k, carry):
+        z = lax.rem(k + 1, planes)
+        swap(z).wait_recv()
+        lines[z] = apply(radial, load_term, z)
+        return carry
+
+    lax.fori_loop(0, planes, forward, 0)
+
+    ratio = line_ref[ph, 0]
+    rising = lines[0]
+    for z in range(1, planes):
+        rising = rising * ratio + lines[z]
+    falling = lines[planes - 1]
+    for z in range(planes - 2, -1, -1):
+        falling = falling * ratio + lines[z]
+    for j in range(blocks):
+        ends_out[j] = rising[8 * j : 8 * j + 8]
+        ends_out[blocks + j] = falling[8 * j : 8 * j + 8]
+
+    def exchange(src, dst, send, recv, hop, sender):
+        to = lax.rem(me + hop, gz_count)
+        at = lax.rem(me + gz_count - hop, gz_count) if sender else me
+        return pltpu.make_async_remote_copy(
+            src_ref=src.at[to],
+            dst_ref=dst.at[at],
+            send_sem=send.at[hop],
+            recv_sem=recv.at[hop],
+            device_id=(to, ph),
+            device_id_type=MESH_ID,
+        )
+
+    for hop in range(1, gz_count):
+        exchange(ends_out, ends_in, ends_send, ends_recv, hop, False).start()
+    ends_in[me] = ends_out[me]
+
+    def flip(l, carry):
+        radial_back[pl.ds(pl.multiple_of(l * rows, rows), rows), :] = radial[
+            pl.ds(l, rows, stride=rows), :
+        ]
+        return carry
+
+    lax.fori_loop(0, rows, flip, 0)
+
+    for hop in range(1, gz_count):
+        exchange(ends_out, ends_in, ends_send, ends_recv, hop, True).wait_recv()
+
+    is_rise = 1 - me // blocks
+    mine = lax.rem(me, blocks)
+    jump = line_ref[ph, 2, pl.ds(pl.multiple_of(mine * 8, 8), 8), :]
+    wrap = line_ref[ph, 3, pl.ds(pl.multiple_of(mine * 8, 8), 8), :]
+    order = [is_rise * s + (1 - is_rise) * (gz_count - 1 - s) for s in range(gz_count)]
+    state = jnp.zeros((8, half), jnp.float32)
+    for s in range(gz_count):
+        state = state * jump + ends_in[order[s]]
+    state = state * wrap
+    for s in range(gz_count):
+        states_out[order[s]] = state
+        state = state * jump + ends_in[order[s]]
+
+    for hop in range(1, gz_count):
+        exchange(states_out, states_in, states_send, states_recv, hop, False).start()
+    states_in[me] = states_out[me]
+    for hop in range(1, gz_count):
+        exchange(states_out, states_in, states_send, states_recv, hop, True).wait_recv()
+
+    scale = line_ref[ph, 1]
+    right = jnp.concatenate([states_in[blocks + j] for j in range(blocks)], 0)
+    left = jnp.concatenate([states_in[j] for j in range(blocks)], 0)
+    solved[planes] = right
+    behind = right * ratio
+    for z in range(planes - 1, -1, -1):
+        solved[z] = behind
+        behind = (behind + lines[z]) * ratio
+    ahead_state = left
+    for z in range(planes):
+        ahead_state = ahead_state * ratio + lines[z]
+        solved[z] = (solved[z] + ahead_state) * scale
+    solved[planes] = (solved[planes] + ahead_state * ratio) * scale
+
+    def give(z, index):
+        return pltpu.make_async_remote_copy(
+            src_ref=result.at[index, z],
+            dst_ref=result.at[index, z],
+            send_sem=back_send.at[z],
+            recv_sem=back_recv.at[z],
+            device_id=(me, other),
+            device_id_type=MESH_ID,
+        )
+
+    def load_solved(z, r):
+        return solved[z, pl.ds(r, 1), :]
+
+    shrink = 1.0 / jnp.sqrt(radii[:, :half])
+
+    def inverse(z, carry):
+        result[ph, z] = apply(radial_back, load_solved, z) * shrink
+        give(z, ph).start()
+        return carry
+
+    lax.fori_loop(0, planes + 1, inverse, 0)
+
+    def finish(z, carry):
+        give(z, other).wait_recv()
+        both = jnp.concatenate([result[0, z], result[1, z]], 1)
+        space[z] = triple_dot(both, back_ref[0], back_ref[1])
+        return carry
+
+    lax.fori_loop(0, planes + 1, finish, 0)
+
+    def correct(z, carry):
+        here = space[z]
+        pressure_ref[z] = here
+        open_radial, open_around, open_axial = opens(z)
+        radial_step = (pltpu.roll(here, rows - 1, 0) - here) * open_radial
+        around_step = (pltpu.roll(here, around - 1, 1) - here) / (radii * angle_step) * open_around
+        axial_step = (space[z + 1] - here) * open_axial
+        for a, step in enumerate((radial_step, around_step, axial_step)):
+            corrected_ref[0, a, z] = (pred[a, z] - DT_STEP * step).astype(jnp.bfloat16)
+        return carry
+
+    lax.fori_loop(0, planes, correct, 0)
+
+    for z in range(planes):
+        swap(z).wait_send()
+    for hop in range(1, gz_count):
+        exchange(ends_out, ends_in, ends_send, ends_recv, hop, False).wait_send()
+        exchange(states_out, states_in, states_send, states_recv, hop, False).wait_send()
+    for z in range(planes + 1):
+        give(z, ph).wait_send()
+
+
+def drum_step(gz_count, frac, velocity, gas_vel, diameters, phase_map, wall_mask, offsets):
+    planes, rows, around = frac.shape[1:]
+    half = around // 2
+    first, nyquist, line, ahead, back = operator_tables(rows, around, offsets.shape[0], planes)
+    smem = pl.BlockSpec(memory_space=pltpu.SMEM)
+    vmem = pl.BlockSpec(memory_space=pltpu.VMEM)
+    f32 = jnp.float32
+    dma = pltpu.SemaphoreType.DMA
+    ends = (gz_count, 8, half)
+    return pl.pallas_call(
+        functools.partial(drum_kernel, gz_count),
+        out_shape=(
+            jax.ShapeDtypeStruct((planes, rows, around), f32),
+            jax.ShapeDtypeStruct((1, 3, planes, rows, around), jnp.bfloat16),
+        ),
+        in_specs=[smem] * 3 + [vmem] * 8 + [pl.BlockSpec(memory_space=pl.ANY)],
+        out_specs=(vmem, vmem),
+        scratch_shapes=[
+            pltpu.VMEM((planes + 1, rows, around), f32),
+            pltpu.VMEM((3, planes, rows, around), f32),
+            pltpu.VMEM((planes, rows, around), f32),
+            pltpu.VMEM((planes + 1, rows, around), f32),
+            pltpu.VMEM((rows, around), f32),
+            pltpu.VMEM((2, planes, rows, half), f32),
+            pltpu.VMEM((planes, rows, half), f32),
+            pltpu.VMEM((rows * rows, half), f32),
+            pltpu.VMEM((rows * rows, half), f32),
+            pltpu.VMEM((planes, rows, half), f32),
+            pltpu.VMEM(ends, f32),
+            pltpu.VMEM(ends, f32),
+            pltpu.VMEM(ends, f32),
+            pltpu.VMEM(ends, f32),
+            pltpu.VMEM((planes + 1, rows, half), f32),
+            pltpu.VMEM((2, planes + 1, rows, half), f32),
+            pltpu.VMEM((planes + 1, rows, around), f32),
+            dma,
+            dma((2,)),
+            dma((planes,)),
+            dma((planes,)),
+            dma((gz_count,)),
+            dma((gz_count,)),
+            dma((gz_count,)),
+            dma((gz_count,)),
+            dma((planes + 1,)),
+            dma((planes + 1,)),
+        ],
+        compiler_params=pltpu.CompilerParams(
+            collective_id=0, has_side_effects=True, vmem_limit_bytes=56 * 1024 * 1024
+        ),
+    )(
+        offsets,
+        diameters,
+        phase_map,
+        frac,
+        velocity,
+        gas_vel,
+        wall_mask,
+        jnp.asarray(nyquist),
+        jnp.asarray(line),
+        jnp.asarray(ahead),
+        jnp.asarray(back),
+        jnp.asarray(first.reshape(rows * rows, half)),
+    )
+
+
 def solution(mesh):
     in_specs = (
         P("ph", "gz", None, None),
@@ -146,4 +586,13 @@
         P(),
     )
     out_specs = (P("gz", None, None), P("ph", None, "gz", None, None))
-    return jax.shard_map(shards, mesh=mesh, in_specs=in_specs, out_specs=out_specs, check_vma=False)
+    gz_count, ph_count = mesh.shape["gz"], mesh.shape["ph"]
+
+    def body(frac, *rest):
+        rows, around = frac.shape[2:]
+        fits = ph_count == 2 and around == 256 and rows <= 128
+        if fits and rows * 2 == gz_count * 8 and frac.shape[1] <= 8:
+            return drum_step(gz_count, frac, *rest)
+        return shards(frac, *rest)
+
+    return jax.shard_map(body, mesh=mesh, in_specs=in_specs, out_specs=out_specs, check_vma=False)

time: 305 us -> 41.5 us (0.14)
  other arithmetic: 162 us -> 0 us
  waiting for transfers between devices: 51.7 us -> 0 us
  local copies, waits for them, and re-layouts: 45.4 us -> 3.96 us
  Pallas kernels: 0 us -> 36 us
  between operations: 17.7 us -> 1.29 us
  starting transfers between devices: 14.9 us -> 0 us
  matrix products: 10.7 us -> 0 us
    div x6 -> x0, other arithmetic: 78.5 us -> none  [the longest x1 77.2 us: radial_solve(): solved = lax.linalg.tridiagonal_solve(lower, diag, upper, right)[..., 0]]
    broadcast_in_dim x2 -> x0, other arithmetic: 63.1 us -> none  [the longest x1 61.8 us: radial_solve(): solved = lax.linalg.tridiagonal_solve(lower, diag, upper, right)[..., 0]]
    pallas_call x0 -> x1, Pallas kernels: none -> 36 us  [drum_step(): pl.pallas_call(functools.partial(drum_kernel, gz_count), out_shape=(jax.S...]
    psum x1 -> x0, waiting for transfers between devices: 24.9 us -> none  [shards(): source = lax.psum(term, 'ph')]
    all_to_all x3 -> x0, waiting for transfers between devices: 21.5 us -> none  [the longest x1 11.4 us: shards(): lax.all_to_all(modes, 'gz', split_axis=2, concat_axis=0, tiled=True)]
    all_to_all x3 -> x0, starting transfers between devices: 14.3 us -> none  [the longest x1 5.62 us: shards(): lax.all_to_all(modes, 'gz', split_axis=2, concat_axis=0, tiled=True)]
    slice x28 -> x0, local copies, waits for them, and re-layouts: 11.7 us -> none  [the longest x13 6.07 us: radial_solve(): solved = lax.linalg.tridiagonal_solve(lower, diag, upper, right)[..., 0]]
    dot_general x5 -> x0, matrix products: 10.7 us -> none  [the longest x2 5.41 us: to_space(): jnp.dot(modes.reshape(-1, around_table.shape[0]), around_table.T, precisi...]
  transfers between devices with their start and end apart: 5 -> 0, of which waited for: 5 -> 0; matrix products, arithmetic and copies ran while one was open for 8% -> 0% of each run, Pallas kernels for 0% -> 0%
where the time goes in v1:
time: 41.5 us; the launch traced here: 41.3 us
  Pallas kernels  36 us (87%)
  local copies, waits for them, and re-layouts  3.96 us (10%)
  between operations  1.29 us (3%)
    pallas_call x1, Pallas kernels, drum_step(): pl.pallas_call(functools.partial(drum_kernel, gz_count), out_shape=(jax.S...  36 us
    unnamed x2, local copies, waits for them, and re-layouts  3.96 us

profile of v1, /device:TPU:0, one launch (start us, length us, event | category | flops | bytes accessed | tf_op | source)
XLA Modules:
  0.0 41.3 jit_solution(10428053897117643914)
XLA Ops:
  1.3 36.0 %shard_map.131 = (f32[8,64,256]{2,1,0:T(8,128)}, bf16[1,3,8,64,256]{4,3,2,1,0:T(8,128)(2,1)}) custom-call(s32[128]{0:T(128)} %offsets_ref.1, f32[32]{0:T(128)} %diameters_ref.1, s32[1]{0:T(128)S(6)} %copy.16.map_ref, bf16[1,8,64,256]{3,2,1,0:T(8,128)(2,1)} %frac_ref.1, bf16[1,3,8,64,256]{4,3,2,1,0:T(8,128)(2,1)} %velocity_ref.1, ...), custom_call_target="tpu_custom_call" | custom-call | tf_op jit(solution)/shard_map/pallas_call | solution.py:522
  37.3 1.9 %copy.17 = f32[8,64,256]{2,1,0:T(8,128)} copy(f32[8,64,256]{2,1,0:T(8,128)} %get-tuple-element.4) | data formatting | bytes 1048576
  39.2 2.1 %copy.18 = bf16[1,3,8,64,256]{4,3,2,1,0:T(8,128)(2,1)} copy(bf16[1,3,8,64,256]{4,3,2,1,0:T(8,128)(2,1)} %get-tuple-element.5) | data formatting | bytes 1572864

commit v2 on v1

--- a/solution.py
+++ b/solution.py
@@ -12,6 +12,7 @@
 DT_STEP = 0.5
 DRAG_SCALE = 20.0
 COMPRESS = 0.005
+CORRECT_STEPS = 2
 HIGHEST = lax.Precision.HIGHEST
 
 
@@ -211,17 +212,26 @@
     offsets_ref,
     diameters_ref,
     map_ref,
+    wall_hbm,
+    frac_hbm,
+    velocity_hbm,
+    gas_hbm,
+    ahead_hbm,
+    nyquist_hbm,
+    line_hbm,
+    back_hbm,
+    radial_hbm,
+    space_out,
+    pred_out,
+    fluid_out,
+    wall_ref,
     frac_ref,
     velocity_ref,
     gas_ref,
-    wall_ref,
+    ahead_ref,
     nyquist_ref,
     line_ref,
-    ahead_ref,
     back_ref,
-    radial_hbm,
-    pressure_ref,
-    corrected_ref,
     fluid,
     pred,
     term,
@@ -240,6 +250,8 @@
     result,
     space,
     table_sem,
+    input_sem,
+    out_sem,
     halo_sem,
     swap_send,
     swap_recv,
@@ -266,8 +278,26 @@
         )
     pl.semaphore_signal(barrier, inc=1, device_id=(me, other), device_id_type=MESH_ID)
 
+    pairs = (
+        (wall_hbm, wall_ref),
+        (frac_hbm, frac_ref),
+        (velocity_hbm, velocity_ref),
+        (gas_hbm, gas_ref),
+        (ahead_hbm, ahead_ref),
+        (nyquist_hbm, nyquist_ref),
+        (line_hbm, line_ref),
+        (back_hbm, back_ref),
+    )
+    fetches = [pltpu.make_async_copy(a, b, input_sem.at[i]) for i, (a, b) in enumerate(pairs)]
     table_copy = pltpu.make_async_copy(radial_hbm, radial, table_sem)
+    for fetch in fetches[:5]:
+        fetch.start()
     table_copy.start()
+    for fetch in fetches[5:]:
+        fetch.start()
+    fluid_copy = pltpu.make_async_copy(fluid, fluid_out, out_sem.at[0])
+    pred_copy = pltpu.make_async_copy(pred, pred_out, out_sem.at[1])
+    fetches[0].wait()
 
     radii = lax.broadcasted_iota(jnp.int32, (rows, around), 0).astype(jnp.float32) + 0.5
     row_id = lax.broadcasted_iota(jnp.int32, (rows, around), 0)
@@ -285,6 +315,9 @@
 
     lax.fori_loop(0, planes + 1, rotate, 0)
 
+    fluid_copy.start()
+    for fetch in fetches[1:4]:
+        fetch.wait()
     size = diameters_ref[map_ref[0]]
     axial_flux[0] = jnp.zeros((rows, around), jnp.float32)
 
@@ -321,6 +354,8 @@
 
     lax.fori_loop(0, planes, source, 0)
 
+    pred_copy.start()
+    fetches[4].wait()
     pl.semaphore_wait(barrier, gz_count)
 
     halo_copy = pltpu.make_async_remote_copy(
@@ -358,6 +393,8 @@
     to_modes(0, term[0] - halo[...] * weight)
 
     table_copy.wait()
+    for fetch in fetches[5:]:
+        fetch.wait()
     is_other = jnp.where(ph == 1, 1, 0)
     lane0 = (lax.broadcasted_iota(jnp.int32, (rows, half), 1) == 0) & (
         jnp.broadcast_to(is_other, (rows, half)) == 1
@@ -484,22 +521,10 @@
         give(z, other).wait_recv()
         both = jnp.concatenate([result[0, z], result[1, z]], 1)
         space[z] = triple_dot(both, back_ref[0], back_ref[1])
+        pltpu.make_async_copy(space.at[z], space_out.at[z], out_sem.at[z + 2]).start()
         return carry
 
     lax.fori_loop(0, planes + 1, finish, 0)
-
-    def correct(z, carry):
-        here = space[z]
-        pressure_ref[z] = here
-        open_radial, open_around, open_axial = opens(z)
-        radial_step = (pltpu.roll(here, rows - 1, 0) - here) * open_radial
-        around_step = (pltpu.roll(here, around - 1, 1) - here) / (radii * angle_step) * open_around
-        axial_step = (space[z + 1] - here) * open_axial
-        for a, step in enumerate((radial_step, around_step, axial_step)):
-            corrected_ref[0, a, z] = (pred[a, z] - DT_STEP * step).astype(jnp.bfloat16)
-        return carry
-
-    lax.fori_loop(0, planes, correct, 0)
 
     for z in range(planes):
         swap(z).wait_send()
@@ -508,6 +533,30 @@
         exchange(states_out, states_in, states_send, states_recv, hop, False).wait_send()
     for z in range(planes + 1):
         give(z, ph).wait_send()
+        pltpu.make_async_copy(space.at[z], space_out.at[z], out_sem.at[z + 2]).wait()
+    fluid_copy.wait()
+    pred_copy.wait()
+
+
+def correct_kernel(space, space_next, pred, fluid, fluid_next, pressure_ref, corrected_ref):
+    count, rows, around = space.shape
+    radii = lax.broadcasted_iota(jnp.int32, (rows, around), 0).astype(jnp.float32) + 0.5
+    row_id = lax.broadcasted_iota(jnp.int32, (rows, around), 0)
+    angle_step = 2.0 * math.pi / around
+    arc = 1.0 / (radii * angle_step)
+    for z in range(count):
+        here = space[z]
+        mask = fluid[z]
+        space_later = space[z + 1] if z + 1 < count else space_next[0]
+        mask_later = fluid[z + 1] if z + 1 < count else fluid_next[0]
+        pressure_ref[z] = here
+        open_radial = jnp.where(row_id == rows - 1, 0.0, mask * pltpu.roll(mask, rows - 1, 0))
+        open_around = mask * pltpu.roll(mask, around - 1, 1)
+        radial_step = (pltpu.roll(here, rows - 1, 0) - here) * open_radial
+        around_step = (pltpu.roll(here, around - 1, 1) - here) * arc * open_around
+        axial_step = (space_later - here) * (mask * mask_later)
+        for a, step in enumerate((radial_step, around_step, axial_step)):
+            corrected_ref[0, a, z] = (pred[a, z] - DT_STEP * step).astype(jnp.bfloat16)
 
 
 def drum_step(gz_count, frac, velocity, gas_vel, diameters, phase_map, wall_mask, offsets):
@@ -515,19 +564,27 @@
     half = around // 2
     first, nyquist, line, ahead, back = operator_tables(rows, around, offsets.shape[0], planes)
     smem = pl.BlockSpec(memory_space=pltpu.SMEM)
-    vmem = pl.BlockSpec(memory_space=pltpu.VMEM)
     f32 = jnp.float32
     dma = pltpu.SemaphoreType.DMA
     ends = (gz_count, 8, half)
-    return pl.pallas_call(
+    space, pred, fluid = pl.pallas_call(
         functools.partial(drum_kernel, gz_count),
         out_shape=(
-            jax.ShapeDtypeStruct((planes, rows, around), f32),
-            jax.ShapeDtypeStruct((1, 3, planes, rows, around), jnp.bfloat16),
+            jax.ShapeDtypeStruct((planes + 1, rows, around), f32),
+            jax.ShapeDtypeStruct((3, planes, rows, around), f32),
+            jax.ShapeDtypeStruct((planes + 1, rows, around), f32),
         ),
-        in_specs=[smem] * 3 + [vmem] * 8 + [pl.BlockSpec(memory_space=pl.ANY)],
-        out_specs=(vmem, vmem),
+        in_specs=[smem] * 3 + [pl.BlockSpec(memory_space=pl.ANY)] * 9,
+        out_specs=[pl.BlockSpec(memory_space=pl.ANY)] * 3,
         scratch_shapes=[
+            pltpu.VMEM(wall_mask.shape, jnp.int32),
+            pltpu.VMEM(frac.shape, jnp.bfloat16),
+            pltpu.VMEM(velocity.shape, jnp.bfloat16),
+            pltpu.VMEM(gas_vel.shape, jnp.bfloat16),
+            pltpu.VMEM(ahead.shape, jnp.bfloat16),
+            pltpu.VMEM(nyquist.shape, f32),
+            pltpu.VMEM(line.shape, f32),
+            pltpu.VMEM(back.shape, jnp.bfloat16),
             pltpu.VMEM((planes + 1, rows, around), f32),
             pltpu.VMEM((3, planes, rows, around), f32),
             pltpu.VMEM((planes, rows, around), f32),
@@ -546,6 +603,8 @@
             pltpu.VMEM((2, planes + 1, rows, half), f32),
             pltpu.VMEM((planes + 1, rows, around), f32),
             dma,
+            dma((8,)),
+            dma((planes + 3,)),
             dma((2,)),
             dma((planes,)),
             dma((planes,)),
@@ -563,16 +622,35 @@
         offsets,
         diameters,
         phase_map,
+        wall_mask,
         frac,
         velocity,
         gas_vel,
-        wall_mask,
+        jnp.asarray(ahead),
         jnp.asarray(nyquist),
         jnp.asarray(line),
-        jnp.asarray(ahead),
         jnp.asarray(back),
         jnp.asarray(first.reshape(rows * rows, half)),
     )
+    chunk = planes // CORRECT_STEPS if planes % CORRECT_STEPS == 0 else planes
+    here = pl.BlockSpec((chunk, rows, around), lambda k: (k, 0, 0))
+    later = pl.BlockSpec((1, rows, around), lambda k: ((k + 1) * chunk, 0, 0))
+    return pl.pallas_call(
+        correct_kernel,
+        grid=(planes // chunk,),
+        out_shape=(
+            jax.ShapeDtypeStruct((planes, rows, around), f32),
+            jax.ShapeDtypeStruct((1, 3, planes, rows, around), jnp.bfloat16),
+        ),
+        in_specs=[
+            here,
+            later,
+            pl.BlockSpec((3, chunk, rows, around), lambda k: (0, k, 0, 0)),
+            here,
+            later,
+        ],
+        out_specs=(here, pl.BlockSpec((1, 3, chunk, rows, around), lambda k: (0, 0, k, 0, 0))),
+    )(space, space, pred, fluid, fluid)
 
 
 def solution(mesh):

time: 41.5 us -> 39 us (0.940)
  local copies, waits for them, and re-layouts: 3.96 us -> 0 us
  Pallas kernels: 36 us -> 37.5 us
    unnamed x2 -> x0, local copies, waits for them, and re-layouts: 3.96 us -> none
    pallas_call x0 -> x1, Pallas kernels: none -> 2.89 us  [drum_step(): pl.pallas_call(correct_kernel, grid=(planes // chunk,), out_shape=(jax.Sh...]
    pallas_call x1, Pallas kernels: 36 us -> 34.6 us  [drum_step(): pl.pallas_call(functools.partial(drum_kernel, gz_count), out_shape=(jax.S...]
where the time goes in v2:
time: 39 us; the launch traced here: 38.8 us
  Pallas kernels  37.5 us (96%)
  between operations  1.29 us (3%)
    pallas_call x1, Pallas kernels, drum_step(): pl.pallas_call(functools.partial(drum_kernel, gz_count), out_shape=(jax.S...  34.6 us
    pallas_call x1, Pallas kernels, drum_step(): pl.pallas_call(correct_kernel, grid=(planes // chunk,), out_shape=(jax.Sh...  2.89 us

profile of v2, /device:TPU:0, one launch (start us, length us, event | category | flops | bytes accessed | tf_op | source)
XLA Modules:
  0.0 38.8 jit_solution(836614237128222456)
XLA Ops:
  1.3 34.6 %shard_map.131 = (f32[9,64,256]{2,1,0:T(8,128)}, f32[3,8,64,256]{3,2,1,0:T(8,128)}, f32[9,64,256]{2,1,0:T(8,128)}) custom-call(s32[128]{0:T(128)} %offsets_ref.1, f32[32]{0:T(128)} %diameters_ref.1, s32[1]{0:T(128)S(6)} %copy.14.map_ref, s32[64,256]{1,0:T(8,128)} %wall_hbm.1, bf16[1,8,64,256]{3,2,1,0:T(8,128)(2,1)} %frac_hbm.1, ...), custom_call_target="tpu_custom_call" | custom-call | tf_op jit(solution)/shard_map/pallas_call | solution.py:570
  35.9 2.9 %shard_map.132 = (f32[8,64,256]{2,1,0:T(8,128)}, bf16[1,3,8,64,256]{4,3,2,1,0:T(8,128)(2,1)}) custom-call(f32[9,64,256]{2,1,0:T(8,128)} %get-tuple-element.5.space.space_next, f32[9,64,256]{2,1,0:T(8,128)} %get-tuple-element.5.space.space_next, f32[3,8,64,256]{3,2,1,0:T(8,128)} %get-tuple-element.6.pred, f32[9,64,256]{2,1,0:T(8,128)} %get-tuple-element.7.fluid.fluid_next, ...), custom_call_target="tpu_custom_call" | custom-call | tf_op jit(solution)/shard_map/pallas_call | solution.py:638
